TPU v7x, 32 devices: a whole 2x2x4 slice. The times are simulated.
32 devices in a mesh: gz: 8 (over z, core), xy: 4 (over y, x).
Axes of the slice: x: 2, y: 2, z: 4, core: 2. Of those that a mesh axis runs over, the one named last changes fastest.
Arguments:
- slab_image: float32 [32, 128, 1024], P('gz', None, 'xy'), may hold values from 0 to 1
- width_taps: float32 [16, 5], replicated, may hold values from -2.5 to 2.5
- height_taps: float32 [16, 5], replicated, may hold values from -2.5 to 2.5
- depth_taps: float32 [16, 5], replicated, may hold values from -2.5 to 2.5
- fragment_ids: int32 [32, 128, 1024], P(None, 'gz', 'xy'), may hold values from 0 to 1023, as said below
- fragment_owner: int32 [32768, 1], P(('gz', 'xy')), may hold values from 0 to 3, as said below
- coarse_centroids: float32 [16, 1024], P(None, ('gz', 'xy')), may hold values from -24 to 24
- parent_map: int32 [4096], P(('gz', 'xy')), may hold values from 0 to 31
- fine_offsets: float32 [16, 4096], P(None, ('gz', 'xy')), may hold values from -2.5 to 2.5
Outputs:
- fragment_means: float32 [16, 32768], P(None, ('gz', 'xy'))
- centroids: float32 [16, 4096], P(None, ('gz', 'xy'))
Inputs may be any that keep to these rules, and one draw needn't show every extreme that they name: `fragment_ids`: ids are local to a pencil block of 32 x 16 x 256 voxels; every id 0 to 1023 occurs in every block. `fragment_owner`: of the 1024 fragments of one pencil block at most 512 name the same owner; in each row along xy some owner takes exactly 512 from every block of that row.
All inputs are finite; a program needn't handle non-finite values.
Results may differ from a plain program's by a relative error of at most 0.00038.
Values may be sent and summed in bfloat16 or wider, within the bound.
A program may use at most 128 MiB of HBM per device.

v0:
```python
import jax
import jax.numpy as jnp
from jax import lax
from jax.sharding import PartitionSpec as P

TAPS = 5
BZ = 4
ITERS = 3
HIGH = lax.Precision.HIGHEST
sharpness = 2.0
group_span = 4


def with_halo(cells, sides, width):
    for axis, dim in sides:
        count = lax.axis_size(axis)
        ends = count - 1
        head = lax.slice_in_dim(cells, 0, width, axis=dim)
        tail = lax.slice_in_dim(cells, cells.shape[dim] - width, cells.shape[dim], axis=dim)
        cells = jnp.concatenate(
            [
                lax.ppermute(tail, axis, [(i, (i + 1) % count) for i in range(ends)]),
                cells,
                lax.ppermute(head, axis, [((i + 1) % count, i) for i in range(ends)]),
            ],
            axis=dim,
        )
    return cells


def planar_filter(padded, width_taps, height_taps):
    reach = width_taps.shape[1]
    rows = padded.shape[1] - reach + 1
    cols = padded.shape[2] - reach + 1
    pieces = []
    for chan_start in range(0, width_taps.shape[0], group_span):
        width_tap = width_taps[chan_start : chan_start + group_span][:, :, None, None, None]
        height_tap = height_taps[chan_start : chan_start + group_span][:, :, None, None, None]
        across = width_tap[:, 0] * padded[None, :, :, 0:cols]
        for tap_shift in range(1, reach):
            across = (
                across + width_tap[:, tap_shift] * padded[None, :, :, tap_shift : tap_shift + cols]
            )
        planar = height_tap[:, 0] * across[:, :, 0:rows, :]
        for tap_shift in range(1, reach):
            planar = (
                planar + height_tap[:, tap_shift] * across[:, :, tap_shift : tap_shift + rows, :]
            )
        pieces.append(planar.astype(jnp.bfloat16))
    return jnp.concatenate(pieces, axis=0)


def depth_filter(planar, depth_taps):
    reach = depth_taps.shape[1]
    half = reach // 2
    depth = planar.shape[1]
    planar = lax.optimization_barrier(planar)
    pieces = []
    for chan_start in range(0, planar.shape[0], group_span):
        block = planar[chan_start : chan_start + group_span].astype(jnp.float32)
        padded = jnp.pad(block, ((0, 0), (half, half), (0, 0), (0, 0)))
        depth_tap = depth_taps[chan_start : chan_start + group_span][:, :, None, None, None]
        response = depth_tap[:, 0] * padded[:, 0:depth]
        for tap_shift in range(1, reach):
            response = response + depth_tap[:, tap_shift] * padded[:, tap_shift : tap_shift + depth]
        pieces.append(jnp.tanh(response).astype(jnp.bfloat16))
    return jnp.concatenate(pieces, axis=0)


def fragment_sums(features, fragment_ids, fragments):
    chans, depth, rows, cols = features.shape
    labels = jnp.arange(fragments, dtype=jnp.int32)
    voxels = BZ * rows * cols

    def add_block(index, carry):
        sums, counts = carry
        start = index * BZ
        block = lax.dynamic_slice_in_dim(features, start, BZ, 1).reshape(chans, voxels)
        block_ids = lax.dynamic_slice_in_dim(fragment_ids, start, BZ, 0).reshape(voxels)
        member = block_ids[:, None] == labels[None, :]
        sums = sums + jnp.dot(
            block, member.astype(jnp.bfloat16), preferred_element_type=jnp.float32
        )
        counts = counts + jnp.sum(member.astype(jnp.float32), axis=0)
        return (sums, counts)

    start_carry = (jnp.zeros((chans, fragments), jnp.float32), jnp.zeros((fragments,), jnp.float32))
    return lax.fori_loop(0, depth // BZ, add_block, start_carry)


def soft_stats(frags, weight, cents):
    cross = lax.dot_general(
        frags, cents, (((0,), (0,)), ((), ())), precision=HIGH, preferred_element_type=jnp.float32
    )
    distance = (
        jnp.sum(frags * frags, axis=0)[:, None]
        + jnp.sum(cents * cents, axis=0)[None, :]
        - 2.0 * cross
    )
    scores = -sharpness * distance
    top = jnp.max(scores, axis=1, keepdims=True)
    expo = jnp.exp(scores - top)
    resp = expo / jnp.sum(expo, axis=1, keepdims=True)
    numer = jnp.dot(
        frags * weight[None, :], resp, precision=HIGH, preferred_element_type=jnp.float32
    )
    denom = jnp.dot(weight[None, :], resp, precision=HIGH, preferred_element_type=jnp.float32)
    return (numer, denom)


def shards(
    slab_image,
    width_taps,
    height_taps,
    depth_taps,
    fragment_ids,
    fragment_owner,
    coarse_centroids,
    parent_map,
    fine_offsets,
):
    half = TAPS // 2
    rimmed = with_halo(slab_image, (("xy", 2),), TAPS // 2)
    rimmed = jnp.pad(rimmed, ((0, 0), (half, half), (0, 0)))
    planar = planar_filter(rimmed, width_taps, height_taps)
    planar = lax.all_to_all(planar, "gz", split_axis=2, concat_axis=1, tiled=True)
    features = depth_filter(planar, depth_taps)
    fragments = fragment_owner.shape[0]
    sums, counts = fragment_sums(features, fragment_ids, fragments)
    means = sums / counts[None, :]
    coarse_count = coarse_centroids.shape[1]
    select = (parent_map[None, :] == jnp.arange(coarse_count, dtype=jnp.int32)[:, None]).astype(
        jnp.float32
    )
    centroids = (
        jnp.dot(coarse_centroids, select, precision=HIGH, preferred_element_type=jnp.float32)
        + fine_offsets
    )
    fine_count = centroids.shape[1]
    pseudo = float(fragment_ids.size // fine_count)
    owner = fragment_owner[:, 0]
    lanes = lax.axis_size("xy")
    capacity = min(fragments // 2, 4 * fragments // lanes)
    pick = (owner[:, None] == jnp.arange(lanes, dtype=jnp.int32)[None, :]).astype(jnp.int32)
    rank = jnp.sum((jnp.cumsum(pick, axis=0) - 1) * pick, axis=1)
    slot = owner * capacity + rank
    packed = jnp.zeros((means.shape[0], lanes * capacity), jnp.float32).at[:, slot].set(means)
    weights = jnp.zeros((1, lanes * capacity), jnp.float32).at[0, slot].set(counts)
    arrived, arrived_weight = (
        lax.all_to_all(packed, "xy", split_axis=1, concat_axis=1, tiled=True),
        lax.all_to_all(weights, "xy", split_axis=1, concat_axis=1, tiled=True),
    )
    for step in range(ITERS):
        numer, denom = soft_stats(arrived, arrived_weight[0], centroids)
        centroids = (numer + pseudo * centroids) / (denom + pseudo)
    return (means, centroids)


def solution(mesh):
    placed = (
        P("gz", None, "xy"),
        P(),
        P(),
        P(),
        P(None, "gz", "xy"),
        P(("gz", "xy"), None),
        P(None, ("gz", "xy")),
        P(("gz", "xy")),
        P(None, ("gz", "xy")),
    )
    return jax.shard_map(
        shards,
        mesh=mesh,
        in_specs=placed,
        out_specs=(P(None, ("gz", "xy")), P(None, ("gz", "xy"))),
        check_vma=False,
    )
```

profile of v0, /device:TPU:0, one launch (start us, length us, event | category | flops | bytes accessed | tf_op | source)
XLA Modules:
  0.0 379.4 jit_solution(12561259763467322268)
XLA Ops:
  0.6 1.2 fusion.109
  1.8 4.9 %collective-permute-start = (f32[4,128,2]{2,1,0:T(8,128)S(1)}, f32[4,128,2]{2,1,0:T(8,128)S(1)}, u32[]{:S(2)}, u32[]{:S(2)}) collective-permute-start(f32[4,128,2]{2,1,0:T(8,128)S(1)} %get-tuple-element.217), channel_id=1, source_target_pairs={{0,1},{1,2},{2,3},{4,5},{5,6},{6,7},{8,9},{9,10},{10,11},{12,13},{... | collective-permute-start | bytes 12296 | tf_op jit(solution)/shard_map/ppermute | solution.py:22
  6.7 1.3 collective-permute-start.1
  12.2 7.6 %collective-permute-done.1 = f32[4,128,2]{2,1,0:T(8,128)S(1)} collective-permute-done((f32[4,128,2]{2,1,0:T(8,128)S(1)}, f32[4,128,2]{2,1,0:T(8,128)S(1)}, u32[]{:S(2)}, u32[]{:S(2)}) %collective-permute-start.1) | collective-permute-done | bytes 4128 | tf_op jit(solution)/shard_map/ppermute | solution.py:24
  19.8 1.4 select_maximum_fusion
  22.9 2.9 multiply_add_fusion.3
  25.8 2.8 fusion.69
  28.6 2.8 fusion.64
  31.4 2.7 multiply_add_fusion.1
  34.1 2.8 fusion.59
  36.9 2.8 fusion.54
  39.7 4.3 %pad_maximum_fusion = bf16[16,4,128,256]{3,1,0,2:T(4,128)(2,1)} fusion(bf16[4,4,128,256]{3,1,0,2:T(4,128)(2,1)S(1)} %fusion.54, bf16[4,4,128,256]{3,1,0,2:T(4,128)(2,1)S(1)} %fusion.59, bf16[4,4,128,256]{3,1,0,2:T(4,128)(2,1)S(1)} %fusion.64, bf16[4,4,128,256]{3,1,0,2:T(4,128)(2,1)S(1)} %fusion.69), kind=kLoop, calls=%fused_computation.12 | loop fusion | flops 6291456 | bytes 8388608 | tf_op jit(solution)/shard_map/concatenate | solution.py:50
  44.1 5.0 %all-to-all-start = ((bf16[16,4,128,256]{3,1,0,2:T(4,128)(2,1)}), bf16[16,4,128,256]{3,1,0,2:T(4,128)(2,1)}, u32[]{:S(2)}, u32[]{:S(2)}) async-start(bf16[16,4,128,256]{3,1,0,2:T(4,128)(2,1)} %pad_maximum_fusion), calls=%async_computation | async-start | bytes 8388608 | tf_op jit(solution)/shard_map/all_to_all | solution.py:126
  49.6 1.1 reduce-window.6
  52.5 90.7 %all-to-all-done = bf16[16,4,128,256]{3,1,0,2:T(4,128)(2,1)} async-done(((bf16[16,4,128,256]{3,1,0,2:T(4,128)(2,1)}), bf16[16,4,128,256]{3,1,0,2:T(4,128)(2,1)}, u32[]{:S(2)}, u32[]{:S(2)}) %all-to-all-start) | async-done | bytes 4194336 | tf_op jit(solution)/shard_map/all_to_all | solution.py:126
  143.2 4.6 %copy.108 = bf16[16,4,128,256]{3,2,1,0:T(8,128)(2,1)S(1)} copy(bf16[16,4,128,256]{3,1,0,2:T(4,128)(2,1)} %all-to-all-done) | data formatting | bytes 8388608 | tf_op jit(solution)/shard_map/all_to_all | solution.py:126
  148.4 1.2 slice_convert_fusion.3
  152.8 2.3 pad_maximum_fusion.1
  155.0 193.2 %while.16 = (s32[]{:T(128)}, f32[16,1024]{1,0:T(8,128)S(1)}, f32[1024]{0:T(1024)S(1)}, bf16[16,32,16,256]{3,2,1,0:T(8,128)(2,1)}, s32[32,16,256]{2,1,0:T(8,128)}...) while((s32[]{:T(128)}, f32[16,1024]{1,0:T(8,128)S(1)}, f32[1024]{0:T(1024)S(1)}, ...), condition=%wide.region_2.3_spmd.clone, body=%wide.region_0.2_spmd.clone.sunk | while | flops 604013568 | bytes 3162270 | solution.py:88
  155.9 1.1 constant_dynamic-slice_fusion.4
  157.3 14.0 %fusion.132 = f32[16,1024]{1,0:T(8,128)S(1)} fusion(bf16[16,16384]{1,0:T(8,128)(2,1)S(1)} %bitcast.93, s32[16384]{0:T(1024)S(1)} %bitcast.96, f32[16,1024]{1,0:T(8,128)S(1)} %get-tuple-element.294, pred[]{:T(512)S(6)} %compare.27), kind=kOutput, calls=%fused_computation.8.clone.1 | convolution fusion | flops 553680896 | bytes 720897 | tf_op jit(solution)/shard_map/while/body/eval_jaxpr/dot_general | solution.py:81
  171.3 7.8 %fusion.133 = f32[1024]{0:T(1024)S(1)} fusion(s32[16384]{0:T(1024)S(1)} %bitcast.97), kind=kLoop, calls=%fused_computation.6.clone.1 | loop fusion | flops 50330624 | bytes 69632 | tf_op jit(solution)/shard_map/while/body/eval_jaxpr/reduce_sum | solution.py:84
  180.1 1.1 constant_dynamic-slice_fusion.4
  181.5 14.0 %fusion.132 = f32[16,1024]{1,0:T(8,128)S(1)} fusion(bf16[16,16384]{1,0:T(8,128)(2,1)S(1)} %bitcast.93, s32[16384]{0:T(1024)S(1)} %bitcast.96, f32[16,1024]{1,0:T(8,128)S(1)} %get-tuple-element.294, pred[]{:T(512)S(6)} %compare.27), kind=kOutput, calls=%fused_computation.8.clone.1 | convolution fusion | flops 553680896 | bytes 720897 | tf_op jit(solution)/shard_map/while/body/eval_jaxpr/dot_general | solution.py:81
  195.5 7.8 %fusion.133 = f32[1024]{0:T(1024)S(1)} fusion(s32[16384]{0:T(1024)S(1)} %bitcast.97), kind=kLoop, calls=%fused_computation.6.clone.1 | loop fusion | flops 50330624 | bytes 69632 | tf_op jit(solution)/shard_map/while/body/eval_jaxpr/reduce_sum | solution.py:84
  204.2 1.1 constant_dynamic-slice_fusion.4
  205.6 14.0 %fusion.132 = f32[16,1024]{1,0:T(8,128)S(1)} fusion(bf16[16,16384]{1,0:T(8,128)(2,1)S(1)} %bitcast.93, s32[16384]{0:T(1024)S(1)} %bitcast.96, f32[16,1024]{1,0:T(8,128)S(1)} %get-tuple-element.294, pred[]{:T(512)S(6)} %compare.27), kind=kOutput, calls=%fused_computation.8.clone.1 | convolution fusion | flops 553680896 | bytes 720897 | tf_op jit(solution)/shard_map/while/body/eval_jaxpr/dot_general | solution.py:81
  219.6 7.8 %fusion.133 = f32[1024]{0:T(1024)S(1)} fusion(s32[16384]{0:T(1024)S(1)} %bitcast.97), kind=kLoop, calls=%fused_computation.6.clone.1 | loop fusion | flops 50330624 | bytes 69632 | tf_op jit(solution)/shard_map/while/body/eval_jaxpr/reduce_sum | solution.py:84
  228.4 1.1 constant_dynamic-slice_fusion.4
  229.8 14.0 %fusion.132 = f32[16,1024]{1,0:T(8,128)S(1)} fusion(bf16[16,16384]{1,0:T(8,128)(2,1)S(1)} %bitcast.93, s32[16384]{0:T(1024)S(1)} %bitcast.96, f32[16,1024]{1,0:T(8,128)S(1)} %get-tuple-element.294, pred[]{:T(512)S(6)} %compare.27), kind=kOutput, calls=%fused_computation.8.clone.1 | convolution fusion | flops 553680896 | bytes 720897 | tf_op jit(solution)/shard_map/while/body/eval_jaxpr/dot_general | solution.py:81
  243.8 7.8 %fusion.133 = f32[1024]{0:T(1024)S(1)} fusion(s32[16384]{0:T(1024)S(1)} %bitcast.97), kind=kLoop, calls=%fused_computation.6.clone.1 | loop fusion | flops 50330624 | bytes 69632 | tf_op jit(solution)/shard_map/while/body/eval_jaxpr/reduce_sum | solution.py:84
  253.9 14.0 %fusion.132 = f32[16,1024]{1,0:T(8,128)S(1)} fusion(bf16[16,16384]{1,0:T(8,128)(2,1)S(1)} %bitcast.93, s32[16384]{0:T(1024)S(1)} %bitcast.96, f32[16,1024]{1,0:T(8,128)S(1)} %get-tuple-element.294, pred[]{:T(512)S(6)} %compare.27), kind=kOutput, calls=%fused_computation.8.clone.1 | convolution fusion | flops 553680896 | bytes 720897 | tf_op jit(solution)/shard_map/while/body/eval_jaxpr/dot_general | solution.py:81
  267.9 7.8 %fusion.133 = f32[1024]{0:T(1024)S(1)} fusion(s32[16384]{0:T(1024)S(1)} %bitcast.97), kind=kLoop, calls=%fused_computation.6.clone.1 | loop fusion | flops 50330624 | bytes 69632 | tf_op jit(solution)/shard_map/while/body/eval_jaxpr/reduce_sum | solution.py:84
  278.1 14.0 %fusion.132 = f32[16,1024]{1,0:T(8,128)S(1)} fusion(bf16[16,16384]{1,0:T(8,128)(2,1)S(1)} %bitcast.93, s32[16384]{0:T(1024)S(1)} %bitcast.96, f32[16,1024]{1,0:T(8,128)S(1)} %get-tuple-element.294, pred[]{:T(512)S(6)} %compare.27), kind=kOutput, calls=%fused_computation.8.clone.1 | convolution fusion | flops 553680896 | bytes 720897 | tf_op jit(solution)/shard_map/while/body/eval_jaxpr/dot_general | solution.py:81
  292.1 7.8 %fusion.133 = f32[1024]{0:T(1024)S(1)} fusion(s32[16384]{0:T(1024)S(1)} %bitcast.97), kind=kLoop, calls=%fused_computation.6.clone.1 | loop fusion | flops 50330624 | bytes 69632 | tf_op jit(solution)/shard_map/while/body/eval_jaxpr/reduce_sum | solution.py:84
  302.2 14.0 %fusion.132 = f32[16,1024]{1,0:T(8,128)S(1)} fusion(bf16[16,16384]{1,0:T(8,128)(2,1)S(1)} %bitcast.93, s32[16384]{0:T(1024)S(1)} %bitcast.96, f32[16,1024]{1,0:T(8,128)S(1)} %get-tuple-element.294, pred[]{:T(512)S(6)} %compare.27), kind=kOutput, calls=%fused_computation.8.clone.1 | convolution fusion | flops 553680896 | bytes 720897 | tf_op jit(solution)/shard_map/while/body/eval_jaxpr/dot_general | solution.py:81
  316.2 7.8 %fusion.133 = f32[1024]{0:T(1024)S(1)} fusion(s32[16384]{0:T(1024)S(1)} %bitcast.97), kind=kLoop, calls=%fused_computation.6.clone.1 | loop fusion | flops 50330624 | bytes 69632 | tf_op jit(solution)/shard_map/while/body/eval_jaxpr/reduce_sum | solution.py:84
  326.4 14.0 %fusion.132 = f32[16,1024]{1,0:T(8,128)S(1)} fusion(bf16[16,16384]{1,0:T(8,128)(2,1)S(1)} %bitcast.93, s32[16384]{0:T(1024)S(1)} %bitcast.96, f32[16,1024]{1,0:T(8,128)S(1)} %get-tuple-element.294, pred[]{:T(512)S(6)} %compare.27), kind=kOutput, calls=%fused_computation.8.clone.1 | convolution fusion | flops 553680896 | bytes 720897 | tf_op jit(solution)/shard_map/while/body/eval_jaxpr/dot_general | solution.py:81
  340.4 7.8 %fusion.133 = f32[1024]{0:T(1024)S(1)} fusion(s32[16384]{0:T(1024)S(1)} %bitcast.97), kind=kLoop, calls=%fused_computation.6.clone.1 | loop fusion | flops 50330624 | bytes 69632 | tf_op jit(solution)/shard_map/while/body/eval_jaxpr/reduce_sum | solution.py:84
  348.4 3.3 scatter_custom_fusion
  352.7 3.6 all-to-all-start.1
  357.0 4.9 %scatter_custom_fusion.1 = f32[2048]{0:T(1024)} fusion(s32[1024]{0:T(1024)S(1)} %broadcast_select_fusion, f32[1024]{0:T(1024)S(1)} %get-tuple-element.113, f32[]{:T(128)} %constant.57.clone.1), kind=kCustom, calls=%fused_computation.182 | custom fusion | bytes 8196
  361.8 3.9 %all-to-all-start.2 = ((f32[1,4,512]{2,0,1:T(1,128)}), f32[1,4,512]{2,0,1:T(1,128)S(1)}, u32[]{:S(2)}, u32[]{:S(2)}) async-start(f32[1,4,512]{2,0,1:T(1,128)} %bitcast.22), calls=%async_computation.2 | async-start | bytes 16384 | tf_op jit(solution)/shard_map/all_to_all | solution.py:151
  365.8 1.2 fusion.113
  367.1 3.3 all-to-all-done.2
  372.3 1.2 fusion.114
  375.6 1.2 fusion.115
  377.9 1.6 fusion.73
  (115 shorter events, 32.7 us)
Async XLA Ops:
  0.6 51.7 %copy-start = (f32[16,32]{1,0:T(8,128)S(1)}, f32[16,32]{1,0:T(8,128)}, u32[]{:S(2)}) copy-start(f32[16,32]{1,0:T(8,128)} %param.17) | copy-start | bytes 6148
  1.8 10.4 %collective-permute-start = (f32[4,128,2]{2,1,0:T(8,128)S(1)}, f32[4,128,2]{2,1,0:T(8,128)S(1)}, u32[]{:S(2)}, u32[]{:S(2)}) collective-permute-start(f32[4,128,2]{2,1,0:T(8,128)S(1)} %get-tuple-element.217), channel_id=1, source_target_pairs={{0,1},{1,2},{2,3},{4,5},{5,6},{6,7},{8,9},{9,10},{10,11},{12,13},{... | collective-permute-start | bytes 12296 | tf_op jit(solution)/shard_map/ppermute | solution.py:22
  6.7 13.1 %collective-permute-start.1 = (f32[4,128,2]{2,1,0:T(8,128)S(1)}, f32[4,128,2]{2,1,0:T(8,128)S(1)}, u32[]{:S(2)}, u32[]{:S(2)}) collective-permute-start(f32[4,128,2]{2,1,0:T(8,128)S(1)} %get-tuple-element.218), channel_id=1, source_target_pairs={{1,0},{2,1},{3,2},{5,4},{6,5},{7,6},{9,8},{10,9},{11,10},{13,12},{... | collective-permute-start | bytes 12296 | tf_op jit(solution)/shard_map/ppermute | solution.py:24
  44.1 5.1 %copy-start.1 = (f32[16,5]{0,1:T(8,128)S(1)}, f32[16,5]{0,1:T(8,128)}, u32[]{:S(2)}) copy-start(f32[16,5]{0,1:T(8,128)} %param.14) | copy-start | bytes 964
  44.1 5.5 %copy-start.2 = (s32[1024,1]{0,1:T(1,128)S(1)}, s32[1024,1]{0,1:T(1,128)}, u32[]{:S(2)}) copy-start(s32[1024,1]{0,1:T(1,128)} %param.16) | copy-start | bytes 12292
  44.1 8.1 %copy-start.5 = (s32[2]{0:T(128)S(1)}, s32[2]{0:T(128)}, u32[]{:S(2)}) copy-start(s32[2]{0:T(128)} %constant.78) | copy-start | bytes 28
  44.1 8.2 %copy-start.6 = (s32[2]{0:T(128)S(1)}, s32[2]{0:T(128)}, u32[]{:S(2)}) copy-start(s32[2]{0:T(128)} %constant.81) | copy-start | bytes 28
  44.1 8.3 %copy-start.3 = (f32[16,128]{1,0:T(8,128)S(1)}, f32[16,128]{1,0:T(8,128)}, u32[]{:S(2)}) copy-start(f32[16,128]{1,0:T(8,128)} %param.19) | copy-start | bytes 24580
  44.1 8.3 %copy-start.4 = (s32[128]{0:T(128)S(1)}, s32[128]{0:T(128)}, u32[]{:S(2)}) copy-start(s32[128]{0:T(128)} %param.18) | copy-start | bytes 1540
  44.1 99.1 %all-to-all-start = ((bf16[16,4,128,256]{3,1,0,2:T(4,128)(2,1)}), bf16[16,4,128,256]{3,1,0,2:T(4,128)(2,1)}, u32[]{:S(2)}, u32[]{:S(2)}) async-start(bf16[16,4,128,256]{3,1,0,2:T(4,128)(2,1)} %pad_maximum_fusion), calls=%async_computation | async-start | bytes 8388608 | tf_op jit(solution)/shard_map/all_to_all | solution.py:126
  352.7 9.1 %all-to-all-start.1 = ((f32[16,4,512]{2,0,1:T(8,128)}), f32[16,4,512]{2,0,1:T(8,128)S(1)}, u32[]{:S(2)}, u32[]{:S(2)}) async-start(f32[16,4,512]{2,0,1:T(8,128)} %copy.114), calls=%async_computation.1 | async-start | bytes 262144 | tf_op jit(solution)/shard_map/all_to_all | solution.py:150
  361.8 8.6 %all-to-all-start.2 = ((f32[1,4,512]{2,0,1:T(1,128)}), f32[1,4,512]{2,0,1:T(1,128)S(1)}, u32[]{:S(2)}, u32[]{:S(2)}) async-start(f32[1,4,512]{2,0,1:T(1,128)} %bitcast.22), calls=%async_computation.2 | async-start | bytes 16384 | tf_op jit(solution)/shard_map/all_to_all | solution.py:151
where the time goes:
time: 381 us; the launch traced here: 379 us
  matrix products  122 us (32%)
  waiting for transfers between devices  102 us (27%)
  other arithmetic  94.4 us (25%)
  local copies, waits for them, and re-layouts  41.2 us (11%)
  starting transfers between devices  18.7 us (5%)
    dot_general x8, matrix products, add_block(): jnp.dot(block, member.astype(jnp.bfloat16), preferred_element_type=jnp.fl...  112 us
    all_to_all x1, waiting for transfers between devices, shards(): lax.all_to_all(planar, 'gz', split_axis=2, concat_axis=1, tiled=True)  90.7 us
    reduce_sum x8, other arithmetic, add_block(): counts = counts + jnp.sum(member.astype(jnp.float32), axis=0)  62.5 us
    convert_element_type x4, other arithmetic, planar_filter(): pieces.append(planar.astype(jnp.bfloat16))  11.2 us
    dynamic_slice x8, local copies, waits for them, and re-layouts, add_block(): lax.dynamic_slice_in_dim(features, start, BZ, 1).reshape(chans, voxels)  8.71 us
  transfers between devices with their start and end apart: 5, of which 4 were waited for; matrix products, arithmetic and copies ran while one was open for 4% of the time, Pallas kernels for 0%

commit v1 on v0

--- a/solution.py
+++ b/solution.py
@@ -2,6 +2,7 @@
 import jax.numpy as jnp
 from jax import lax
 from jax.sharding import PartitionSpec as P
+from jax.lax import axis_index, ppermute, psum
 
 TAPS = 5
 BZ = 4
@@ -123,7 +124,27 @@
     rimmed = with_halo(slab_image, (("xy", 2),), TAPS // 2)
     rimmed = jnp.pad(rimmed, ((0, 0), (half, half), (0, 0)))
     planar = planar_filter(rimmed, width_taps, height_taps)
-    planar = lax.all_to_all(planar, "gz", split_axis=2, concat_axis=1, tiled=True)
+
+    def define_classes_for(slab_in, shard_axis):
+        res = psum(1, shard_axis)
+        side_arr = axis_index(shard_axis)
+        newest, block_last = (res, side_arr)
+        left_arr = slab_in.shape[2] // newest
+        carry_in = list(slab_in.shape)
+        carry_in[2] = left_arr
+        y_new = carry_in[1]
+        carry_in[1] = y_new * newest
+        taken_in = jnp.zeros(carry_in, slab_in.dtype)
+        for dev in range(newest):
+            tmp = lax.dynamic_slice_in_dim(slab_in, (block_last ^ dev) * left_arr, left_arr, axis=2)
+            if dev:
+                tmp = ppermute(tmp, shard_axis, [(b, b ^ dev) for b in range(newest)])
+            taken_in = lax.dynamic_update_slice_in_dim(
+                taken_in, tmp, (block_last ^ dev) * y_new, axis=1
+            )
+        return taken_in
+
+    planar = define_classes_for(planar, "gz")
     features = depth_filter(planar, depth_taps)
     fragments = fragment_owner.shape[0]
     sums, counts = fragment_sums(features, fragment_ids, fragments)

time: 381 us -> 366 us (0.961)
  the two profiles are of different devices: /device:TPU:0 before, /device:TPU:16 now
where the time goes in v1:
time: 366 us; the launch traced here: 364 us
  matrix products  123 us (34%)
  waiting for transfers between devices  88 us (24%)
  other arithmetic  87.5 us (24%)
  local copies, waits for them, and re-layouts  46 us (13%)
  starting transfers between devices  18.7 us (5%)
    dot_general x8, matrix products, add_block(): jnp.dot(block, member.astype(jnp.bfloat16), preferred_element_type=jnp.fl...  112 us
    ppermute x7, waiting for transfers between devices, define_classes_for(): tmp = ppermute(tmp, shard_axis, [(b, b ^ dev) for b in range(newest)])  84 us
    reduce_sum x8, other arithmetic, add_block(): counts = counts + jnp.sum(member.astype(jnp.float32), axis=0)  62.5 us
    dynamic_slice x8, local copies, waits for them, and re-layouts, add_block(): lax.dynamic_slice_in_dim(features, start, BZ, 1).reshape(chans, voxels)  8.71 us
  transfers between devices with their start and end apart: 11, of which 7 were waited for; matrix products, arithmetic and copies ran while one was open for 7% of the time, Pallas kernels for 0%

profile of v1, /device:TPU:16, one launch (start us, length us, event | category | flops | bytes accessed | tf_op | source)
XLA Modules:
  0.0 364.4 jit_solution(8025099707867173564)
XLA Ops:
  0.6 1.2 fusion.109
  1.8 3.4 collective-permute-start
  5.2 1.3 collective-permute-start.1
  11.4 1.1 reduce-window.6
  18.3 1.4 select_maximum_fusion
  20.4 1.4 multiply_add_fusion.3
  21.8 1.3 fusion.69
  23.0 1.3 fusion.64
  24.3 1.4 multiply_add_fusion.1
  25.7 1.3 fusion.59
  27.0 1.3 fusion.54
  29.0 2.3 broadcast_in_dim.40
  31.4 2.0 constant_dynamic-slice_fusion.2
  33.6 1.6 collective-permute-start.3
  36.7 2.2 collective-permute-start.6
  40.6 26.2 %collective-permute-done.3 = bf16[16,4,16,256]{3,2,1,0:T(8,128)(2,1)S(1)} collective-permute-done((bf16[16,4,16,256]{3,2,1,0:T(8,128)(2,1)}, bf16[16,4,16,256]{3,2,1,0:T(8,128)(2,1)S(1)}, u32[]{:S(2)}, u32[]{:S(2)}) %collective-permute-start.3) | collective-permute-done | bytes 524320 | tf_op jit(solution)/shard_map/ppermute | solution.py:141
  68.2 9.5 %collective-permute-done.4 = bf16[16,4,16,256]{3,2,1,0:T(8,128)(2,1)S(1)} collective-permute-done((bf16[16,4,16,256]{3,2,1,0:T(8,128)(2,1)}, bf16[16,4,16,256]{3,2,1,0:T(8,128)(2,1)S(1)}, u32[]{:S(2)}, u32[]{:S(2)}) %collective-permute-start.4) | collective-permute-done | bytes 524320 | tf_op jit(solution)/shard_map/ppermute | solution.py:141
  79.4 25.8 %collective-permute-done.6 = bf16[16,4,16,256]{3,2,1,0:T(8,128)(2,1)S(1)} collective-permute-done((bf16[16,4,16,256]{3,2,1,0:T(8,128)(2,1)}, bf16[16,4,16,256]{3,2,1,0:T(8,128)(2,1)S(1)}, u32[]{:S(2)}, u32[]{:S(2)}) %collective-permute-start.6) | collective-permute-done | bytes 524320 | tf_op jit(solution)/shard_map/ppermute | solution.py:141
  106.0 13.4 %collective-permute-done.7 = bf16[16,4,16,256]{3,2,1,0:T(8,128)(2,1)S(1)} collective-permute-done((bf16[16,4,16,256]{3,2,1,0:T(8,128)(2,1)}, bf16[16,4,16,256]{3,2,1,0:T(8,128)(2,1)S(1)}, u32[]{:S(2)}, u32[]{:S(2)}) %collective-permute-start.7) | collective-permute-done | bytes 524320 | tf_op jit(solution)/shard_map/ppermute | solution.py:141
  120.3 9.1 %collective-permute-done.8 = bf16[16,4,16,256]{3,2,1,0:T(8,128)(2,1)S(1)} collective-permute-done((bf16[16,4,16,256]{3,2,1,0:T(8,128)(2,1)S(1)}, bf16[16,4,16,256]{3,2,1,0:T(8,128)(2,1)S(1)}, u32[]{:S(2)}, u32[]{:S(2)}) %collective-permute-start.8) | collective-permute-done | bytes 524320 | tf_op jit(solution)/shard_map/ppermute | solution.py:141
  130.2 3.3 slice_convert_fusion.3
  136.7 2.3 pad_maximum_fusion.1
  139.0 193.2 %while.16 = (s32[]{:T(128)}, f32[16,1024]{1,0:T(8,128)S(1)}, f32[1024]{0:T(1024)S(1)}, bf16[16,32,16,256]{3,2,1,0:T(8,128)(2,1)}, s32[32,16,256]{2,1,0:T(8,128)}...) while((s32[]{:T(128)}, f32[16,1024]{1,0:T(8,128)S(1)}, f32[1024]{0:T(1024)S(1)}, ...), condition=%wide.region_2.3_spmd.clone, body=%wide.region_0.2_spmd.clone.sunk | while | flops 604013568 | bytes 3162270 | solution.py:89
  141.3 14.0 %fusion.132 = f32[16,1024]{1,0:T(8,128)S(1)} fusion(bf16[16,16384]{1,0:T(8,128)(2,1)S(1)} %bitcast.87, s32[16384]{0:T(1024)S(1)} %bitcast.90, f32[16,1024]{1,0:T(8,128)S(1)} %get-tuple-element.302, pred[]{:T(512)S(6)} %compare.27), kind=kOutput, calls=%fused_computation.8.clone.1 | convolution fusion | flops 553680896 | bytes 720897 | tf_op jit(solution)/shard_map/while/body/eval_jaxpr/dot_general | solution.py:82
  155.3 7.8 %fusion.133 = f32[1024]{0:T(1024)S(1)} fusion(s32[16384]{0:T(1024)S(1)} %bitcast.91), kind=kLoop, calls=%fused_computation.6.clone.1 | loop fusion | flops 50330624 | bytes 69632 | tf_op jit(solution)/shard_map/while/body/eval_jaxpr/reduce_sum | solution.py:85
  165.4 14.0 %fusion.132 = f32[16,1024]{1,0:T(8,128)S(1)} fusion(bf16[16,16384]{1,0:T(8,128)(2,1)S(1)} %bitcast.87, s32[16384]{0:T(1024)S(1)} %bitcast.90, f32[16,1024]{1,0:T(8,128)S(1)} %get-tuple-element.302, pred[]{:T(512)S(6)} %compare.27), kind=kOutput, calls=%fused_computation.8.clone.1 | convolution fusion | flops 553680896 | bytes 720897 | tf_op jit(solution)/shard_map/while/body/eval_jaxpr/dot_general | solution.py:82
  179.4 7.8 %fusion.133 = f32[1024]{0:T(1024)S(1)} fusion(s32[16384]{0:T(1024)S(1)} %bitcast.91), kind=kLoop, calls=%fused_computation.6.clone.1 | loop fusion | flops 50330624 | bytes 69632 | tf_op jit(solution)/shard_map/while/body/eval_jaxpr/reduce_sum | solution.py:85
  189.6 14.0 %fusion.132 = f32[16,1024]{1,0:T(8,128)S(1)} fusion(bf16[16,16384]{1,0:T(8,128)(2,1)S(1)} %bitcast.87, s32[16384]{0:T(1024)S(1)} %bitcast.90, f32[16,1024]{1,0:T(8,128)S(1)} %get-tuple-element.302, pred[]{:T(512)S(6)} %compare.27), kind=kOutput, calls=%fused_computation.8.clone.1 | convolution fusion | flops 553680896 | bytes 720897 | tf_op jit(solution)/shard_map/while/body/eval_jaxpr/dot_general | solution.py:82
  203.6 7.8 %fusion.133 = f32[1024]{0:T(1024)S(1)} fusion(s32[16384]{0:T(1024)S(1)} %bitcast.91), kind=kLoop, calls=%fused_computation.6.clone.1 | loop fusion | flops 50330624 | bytes 69632 | tf_op jit(solution)/shard_map/while/body/eval_jaxpr/reduce_sum | solution.py:85
  213.7 14.0 %fusion.132 = f32[16,1024]{1,0:T(8,128)S(1)} fusion(bf16[16,16384]{1,0:T(8,128)(2,1)S(1)} %bitcast.87, s32[16384]{0:T(1024)S(1)} %bitcast.90, f32[16,1024]{1,0:T(8,128)S(1)} %get-tuple-element.302, pred[]{:T(512)S(6)} %compare.27), kind=kOutput, calls=%fused_computation.8.clone.1 | convolution fusion | flops 553680896 | bytes 720897 | tf_op jit(solution)/shard_map/while/body/eval_jaxpr/dot_general | solution.py:82
  227.7 7.8 %fusion.133 = f32[1024]{0:T(1024)S(1)} fusion(s32[16384]{0:T(1024)S(1)} %bitcast.91), kind=kLoop, calls=%fused_computation.6.clone.1 | loop fusion | flops 50330624 | bytes 69632 | tf_op jit(solution)/shard_map/while/body/eval_jaxpr/reduce_sum | solution.py:85
  237.9 14.0 %fusion.132 = f32[16,1024]{1,0:T(8,128)S(1)} fusion(bf16[16,16384]{1,0:T(8,128)(2,1)S(1)} %bitcast.87, s32[16384]{0:T(1024)S(1)} %bitcast.90, f32[16,1024]{1,0:T(8,128)S(1)} %get-tuple-element.302, pred[]{:T(512)S(6)} %compare.27), kind=kOutput, calls=%fused_computation.8.clone.1 | convolution fusion | flops 553680896 | bytes 720897 | tf_op jit(solution)/shard_map/while/body/eval_jaxpr/dot_general | solution.py:82
  251.9 7.8 %fusion.133 = f32[1024]{0:T(1024)S(1)} fusion(s32[16384]{0:T(1024)S(1)} %bitcast.91), kind=kLoop, calls=%fused_computation.6.clone.1 | loop fusion | flops 50330624 | bytes 69632 | tf_op jit(solution)/shard_map/while/body/eval_jaxpr/reduce_sum | solution.py:85
  262.0 14.0 %fusion.132 = f32[16,1024]{1,0:T(8,128)S(1)} fusion(bf16[16,16384]{1,0:T(8,128)(2,1)S(1)} %bitcast.87, s32[16384]{0:T(1024)S(1)} %bitcast.90, f32[16,1024]{1,0:T(8,128)S(1)} %get-tuple-element.302, pred[]{:T(512)S(6)} %compare.27), kind=kOutput, calls=%fused_computation.8.clone.1 | convolution fusion | flops 553680896 | bytes 720897 | tf_op jit(solution)/shard_map/while/body/eval_jaxpr/dot_general | solution.py:82
  276.0 7.8 %fusion.133 = f32[1024]{0:T(1024)S(1)} fusion(s32[16384]{0:T(1024)S(1)} %bitcast.91), kind=kLoop, calls=%fused_computation.6.clone.1 | loop fusion | flops 50330624 | bytes 69632 | tf_op jit(solution)/shard_map/while/body/eval_jaxpr/reduce_sum | solution.py:85
  286.2 14.0 %fusion.132 = f32[16,1024]{1,0:T(8,128)S(1)} fusion(bf16[16,16384]{1,0:T(8,128)(2,1)S(1)} %bitcast.87, s32[16384]{0:T(1024)S(1)} %bitcast.90, f32[16,1024]{1,0:T(8,128)S(1)} %get-tuple-element.302, pred[]{:T(512)S(6)} %compare.27), kind=kOutput, calls=%fused_computation.8.clone.1 | convolution fusion | flops 553680896 | bytes 720897 | tf_op jit(solution)/shard_map/while/body/eval_jaxpr/dot_general | solution.py:82
  300.2 7.8 %fusion.133 = f32[1024]{0:T(1024)S(1)} fusion(s32[16384]{0:T(1024)S(1)} %bitcast.91), kind=kLoop, calls=%fused_computation.6.clone.1 | loop fusion | flops 50330624 | bytes 69632 | tf_op jit(solution)/shard_map/while/body/eval_jaxpr/reduce_sum | solution.py:85
  310.3 14.0 %fusion.132 = f32[16,1024]{1,0:T(8,128)S(1)} fusion(bf16[16,16384]{1,0:T(8,128)(2,1)S(1)} %bitcast.87, s32[16384]{0:T(1024)S(1)} %bitcast.90, f32[16,1024]{1,0:T(8,128)S(1)} %get-tuple-element.302, pred[]{:T(512)S(6)} %compare.27), kind=kOutput, calls=%fused_computation.8.clone.1 | convolution fusion | flops 553680896 | bytes 720897 | tf_op jit(solution)/shard_map/while/body/eval_jaxpr/dot_general | solution.py:82
  324.3 7.8 %fusion.133 = f32[1024]{0:T(1024)S(1)} fusion(s32[16384]{0:T(1024)S(1)} %bitcast.91), kind=kLoop, calls=%fused_computation.6.clone.1 | loop fusion | flops 50330624 | bytes 69632 | tf_op jit(solution)/shard_map/while/body/eval_jaxpr/reduce_sum | solution.py:85
  332.4 3.3 scatter_custom_fusion
  336.7 4.2 %all-to-all-start = ((f32[16,4,512]{2,0,1:T(8,128)}), f32[16,4,512]{2,0,1:T(8,128)S(1)}, u32[]{:S(2)}, u32[]{:S(2)}) async-start(f32[16,4,512]{2,0,1:T(8,128)} %copy.79), calls=%async_computation | async-start | bytes 262144 | tf_op jit(solution)/shard_map/all_to_all | solution.py:171
  341.6 4.9 %scatter_custom_fusion.1 = f32[2048]{0:T(1024)} fusion(s32[1024]{0:T(1024)S(1)} %broadcast_select_fusion, f32[1024]{0:T(1024)S(1)} %get-tuple-element.113, f32[]{:T(128)} %constant.72.clone.1), kind=kCustom, calls=%fused_computation.183 | custom fusion | bytes 8196
  346.5 4.2 %all-to-all-start.1 = ((f32[1,4,512]{2,0,1:T(1,128)}), f32[1,4,512]{2,0,1:T(1,128)S(1)}, u32[]{:S(2)}, u32[]{:S(2)}) async-start(f32[1,4,512]{2,0,1:T(1,128)} %bitcast.19), calls=%async_computation.1 | async-start | bytes 16384 | tf_op jit(solution)/shard_map/all_to_all | solution.py:172
  350.7 1.2 fusion.113
  352.1 3.3 all-to-all-done.1
  357.3 1.2 fusion.114
  360.5 1.2 fusion.115
  362.8 1.6 fusion.73
  (117 shorter events, 49.2 us)
Async XLA Ops:
  0.6 15.9 %copy-start = (f32[16,32]{1,0:T(8,128)S(1)}, f32[16,32]{1,0:T(8,128)}, u32[]{:S(2)}) copy-start(f32[16,32]{1,0:T(8,128)} %param.17) | copy-start | bytes 6148
  1.8 15.9 %collective-permute-start = (f32[4,128,2]{2,1,0:T(8,128)S(1)}, f32[4,128,2]{2,1,0:T(8,128)S(1)}, u32[]{:S(2)}, u32[]{:S(2)}) collective-permute-start(f32[4,128,2]{2,1,0:T(8,128)S(1)} %get-tuple-element.225), channel_id=1, source_target_pairs={{0,1},{1,2},{2,3},{4,5},{5,6},{6,7},{8,9},{9,10},{10,11},{12,13},{... | collective-permute-start | bytes 12296 | tf_op jit(solution)/shard_map/ppermute | solution.py:23
  5.2 13.1 %collective-permute-start.1 = (f32[4,128,2]{2,1,0:T(8,128)S(1)}, f32[4,128,2]{2,1,0:T(8,128)S(1)}, u32[]{:S(2)}, u32[]{:S(2)}) collective-permute-start(f32[4,128,2]{2,1,0:T(8,128)S(1)} %get-tuple-element.226), channel_id=1, source_target_pairs={{1,0},{2,1},{3,2},{5,4},{6,5},{7,6},{9,8},{10,9},{11,10},{13,12},{... | collective-permute-start | bytes 12296 | tf_op jit(solution)/shard_map/ppermute | solution.py:25
  33.4 5.8 %collective-permute-start.2 = (bf16[16,4,16,256]{3,2,1,0:T(8,128)(2,1)}, bf16[16,4,16,256]{3,2,1,0:T(8,128)(2,1)S(1)}, u32[]{:S(2)}, u32[]{:S(2)}) collective-permute-start(bf16[16,4,16,256]{3,2,1,0:T(8,128)(2,1)} %get-tuple-element.214), channel_id=1, source_target_pairs={{0,4},{4,0},{8,12},{12,8},{16,20},{20,16},{24,28},{28,24},{1,5},{5... | collective-permute-start | bytes 1572872 | tf_op jit(solution)/shard_map/ppermute | solution.py:141
  33.6 33.3 %collective-permute-start.3 = (bf16[16,4,16,256]{3,2,1,0:T(8,128)(2,1)}, bf16[16,4,16,256]{3,2,1,0:T(8,128)(2,1)S(1)}, u32[]{:S(2)}, u32[]{:S(2)}) collective-permute-start(bf16[16,4,16,256]{3,2,1,0:T(8,128)(2,1)} %get-tuple-element.213), channel_id=1, source_target_pairs={{0,8},{4,12},{8,0},{12,4},{16,24},{20,28},{24,16},{28,20},{1,9},{5... | collective-permute-start | bytes 1572872 | tf_op jit(solution)/shard_map/ppermute | solution.py:141
  35.4 42.3 %collective-permute-start.4 = (bf16[16,4,16,256]{3,2,1,0:T(8,128)(2,1)}, bf16[16,4,16,256]{3,2,1,0:T(8,128)(2,1)S(1)}, u32[]{:S(2)}, u32[]{:S(2)}) collective-permute-start(bf16[16,4,16,256]{3,2,1,0:T(8,128)(2,1)} %get-tuple-element.212), channel_id=1, source_target_pairs={{0,12},{4,8},{8,4},{12,0},{16,28},{20,24},{24,20},{28,16},{1,13},{... | collective-permute-start | bytes 1572872 | tf_op jit(solution)/shard_map/ppermute | solution.py:141
  36.0 42.5 %collective-permute-start.5 = (bf16[16,4,16,256]{3,2,1,0:T(8,128)(2,1)}, bf16[16,4,16,256]{3,2,1,0:T(8,128)(2,1)S(1)}, u32[]{:S(2)}, u32[]{:S(2)}) collective-permute-start(bf16[16,4,16,256]{3,2,1,0:T(8,128)(2,1)} %get-tuple-element.211), channel_id=1, source_target_pairs={{0,16},{4,20},{8,24},{12,28},{16,0},{20,4},{24,8},{28,12},{1,17},{... | collective-permute-start | bytes 1572872 | tf_op jit(solution)/shard_map/ppermute | solution.py:141
  36.7 68.5 %collective-permute-start.6 = (bf16[16,4,16,256]{3,2,1,0:T(8,128)(2,1)}, bf16[16,4,16,256]{3,2,1,0:T(8,128)(2,1)S(1)}, u32[]{:S(2)}, u32[]{:S(2)}) collective-permute-start(bf16[16,4,16,256]{3,2,1,0:T(8,128)(2,1)} %get-tuple-element.210), channel_id=1, source_target_pairs={{0,20},{4,16},{8,28},{12,24},{16,4},{20,0},{24,12},{28,8},{1,21},{... | collective-permute-start | bytes 1572872 | tf_op jit(solution)/shard_map/ppermute | solution.py:141
  39.2 80.3 %collective-permute-start.7 = (bf16[16,4,16,256]{3,2,1,0:T(8,128)(2,1)}, bf16[16,4,16,256]{3,2,1,0:T(8,128)(2,1)S(1)}, u32[]{:S(2)}, u32[]{:S(2)}) collective-permute-start(bf16[16,4,16,256]{3,2,1,0:T(8,128)(2,1)} %get-tuple-element.209), channel_id=1, source_target_pairs={{0,24},{4,28},{8,16},{12,20},{16,8},{20,12},{24,0},{28,4},{1,25},{... | collective-permute-start | bytes 1572872 | tf_op jit(solution)/shard_map/ppermute | solution.py:141
  66.9 62.6 %collective-permute-start.8 = (bf16[16,4,16,256]{3,2,1,0:T(8,128)(2,1)S(1)}, bf16[16,4,16,256]{3,2,1,0:T(8,128)(2,1)S(1)}, u32[]{:S(2)}, u32[]{:S(2)}) collective-permute-start(bf16[16,4,16,256]{3,2,1,0:T(8,128)(2,1)S(1)} %get-tuple-element.208), channel_id=1, source_target_pairs={{0,28},{4,24},{8,20},{12,16},{16,12},{20,8},{24,4},{28,0},{1,29},{... | collective-permute-start | bytes 1572872 | tf_op jit(solution)/shard_map/ppermute | solution.py:141
  336.7 9.8 %all-to-all-start = ((f32[16,4,512]{2,0,1:T(8,128)}), f32[16,4,512]{2,0,1:T(8,128)S(1)}, u32[]{:S(2)}, u32[]{:S(2)}) async-start(f32[16,4,512]{2,0,1:T(8,128)} %copy.79), calls=%async_computation | async-start | bytes 262144 | tf_op jit(solution)/shard_map/all_to_all | solution.py:171
  346.5 8.9 %all-to-all-start.1 = ((f32[1,4,512]{2,0,1:T(1,128)}), f32[1,4,512]{2,0,1:T(1,128)S(1)}, u32[]{:S(2)}, u32[]{:S(2)}) async-start(f32[1,4,512]{2,0,1:T(1,128)} %bitcast.19), calls=%async_computation.1 | async-start | bytes 16384 | tf_op jit(solution)/shard_map/all_to_all | solution.py:172
